TPU v7x, 32 devices: a whole 2x2x4 slice. The times are simulated.
32 devices in a mesh: dp: 8 (over y, x, core), seq: 4 (over z).
Axes of the slice: x: 2, y: 2, z: 4, core: 2. Of those that a mesh axis runs over, the one named last changes fastest.
Arguments:
- qkv: bfloat16 [16, 1024, 4608], P('dp', 'seq'), may hold values from -20.4 to 20.4
- gate: float32 [16, 3072], P('dp'), may hold values from 0.5 to 2.5
- cotangent: bfloat16 [16, 1024, 3072], P('dp', 'seq'), may hold values from -6 to 6
- out_weight: bfloat16 [1536, 3072], replicated, may hold values from -0.15625 to 0.15625
- clip_lengths: int32 [16], replicated, may hold values from 1 to 768, as said below
- text_lengths: int32 [16], replicated, may hold values from 1 to 256, as said below
- plan: int32 [8], replicated, may hold values from 0 to 7, as said below
Outputs:
- mixed: bfloat16 [16, 1024, 3072], P('dp', 'seq')
- gate_grad: float32 [16, 3072], P('dp')
- weight_grad: float32 [1536, 3072], P(None, ('dp', 'seq'))
- qkv_grad: bfloat16 [16, 1024, 4608], P('dp', 'seq')
Inputs may be any that keep to these rules, and one draw needn't show every extreme that they name: clip_lengths[c] counts the live video positions of source clip c = 2 g + s (group g, slot s); some clip has exactly 768. text_lengths[c] counts the live text positions of source clip c; some clip has exactly 256. plan is a permutation of 0 to 7: the second clip of group g becomes the second clip of group plan[g].
All inputs are finite; a program needn't handle non-finite values.
Results may differ from a plain program's by a relative error of at most 0.011.
Values may be sent and summed in bfloat16 or wider, within the bound.
A program may use at most 128 MiB of HBM per device.

v0:
```python
import jax
import jax.numpy as jnp
from jax import lax
from jax.sharding import PartitionSpec as P

HD = 128
TXT = 256
BLOCK = 512
NEGATIVE = -1e30


def allowed_rows(offset, count, text_len, video_len):
    places = offset + jnp.arange(count, dtype=jnp.int32)
    return (places < text_len) | (places >= TXT) & (places < TXT + video_len)


def move_in(block_rows, inverse):
    groups = lax.axis_size("dp")
    portions = block_rows.reshape(groups, block_rows.shape[0] // groups, block_rows.shape[1])
    spread = lax.all_to_all(portions, "dp", split_axis=0, concat_axis=0, tiled=True)
    arranged = jnp.take(spread, inverse, axis=0)
    landed = lax.all_to_all(arranged, "dp", split_axis=0, concat_axis=0, tiled=True)
    return landed.reshape(block_rows.shape)


def move_out(block_rows, plan):
    groups = lax.axis_size("dp")
    portions = block_rows.reshape(groups, block_rows.shape[0] // groups, block_rows.shape[1])
    spread = lax.all_to_all(portions, "dp", split_axis=0, concat_axis=0, tiled=True)
    arranged = jnp.take(spread, plan, axis=0)
    landed = lax.all_to_all(arranged, "dp", split_axis=0, concat_axis=0, tiled=True)
    return landed.reshape(block_rows.shape)


def to_heads(tokens, seq_ways):
    clip_count, row_count, full_width = tokens.shape
    local_width = full_width // (3 * seq_ways)
    parted = tokens.reshape(clip_count, row_count, 3, seq_ways, local_width)
    exchanged = lax.all_to_all(parted, "seq", split_axis=3, concat_axis=1, tiled=True)
    return exchanged.reshape(clip_count, row_count * seq_ways, 3, local_width)


def block_scores(query_rows, key_rows, query_ok, key_ok, score_scale):
    scores = (
        jnp.einsum("qhd,khd->hqk", query_rows, key_rows, preferred_element_type=jnp.float32)
        * score_scale
    )
    live_pairs = query_ok[None, :, None] & key_ok[None, None, :]
    return (scores, live_pairs)


def attend(queries, keys_all, values_all, text_len, video_len, score_scale):
    seq_len, head_count, head_dim = queries.shape
    block_count = (TXT + video_len + BLOCK - 1) // BLOCK

    def query_step(query_block, built):
        results, log_totals = built
        offset = query_block * BLOCK
        query_rows = lax.dynamic_slice_in_dim(queries, offset, BLOCK, 0)
        query_ok = allowed_rows(offset, BLOCK, text_len, video_len)

        def scored(key_block):
            key_offset = key_block * BLOCK
            key_rows = lax.dynamic_slice_in_dim(keys_all, key_offset, BLOCK, 0)
            key_ok = allowed_rows(key_offset, BLOCK, text_len, video_len)
            scores, live_pairs = block_scores(query_rows, key_rows, query_ok, key_ok, score_scale)
            return (scores, live_pairs, key_offset)

        def stats_step(key_block, running):
            row_peak, row_total = running
            scores, live_pairs, key_offset = scored(key_block)
            masked = jnp.where(live_pairs, scores, NEGATIVE)
            new_peak = jnp.maximum(row_peak, jnp.max(masked, axis=-1))
            row_total = row_total * jnp.exp(row_peak - new_peak) + jnp.sum(
                jnp.exp(masked - new_peak[..., None]), axis=-1
            )
            return (new_peak, row_total)

        start_peak = jnp.full((head_count, BLOCK), NEGATIVE, jnp.float32)
        row_peak, row_total = lax.fori_loop(
            0, block_count, stats_step, (start_peak, jnp.zeros((head_count, BLOCK), jnp.float32))
        )
        log_total = row_peak + jnp.log(row_total)

        def value_step(key_block, partial_sums):
            scores, live_pairs, key_offset = scored(key_block)
            probs_low = jnp.exp(
                jnp.where(live_pairs, scores - log_total[..., None], NEGATIVE)
            ).astype(jnp.bfloat16)
            value_rows = lax.dynamic_slice_in_dim(values_all, key_offset, BLOCK, 0)
            return partial_sums + jnp.einsum(
                "hqk,khd->qhd", probs_low, value_rows, preferred_element_type=jnp.float32
            )

        partial_sums = lax.fori_loop(
            0, block_count, value_step, jnp.zeros((BLOCK, head_count, head_dim), jnp.float32)
        )
        results = lax.dynamic_update_slice_in_dim(
            results, partial_sums.astype(jnp.bfloat16), offset, 0
        )
        log_totals = lax.dynamic_update_slice_in_dim(log_totals, log_total, offset, 1)
        return (results, log_totals)

    initial = (
        jnp.zeros((seq_len, head_count, head_dim), jnp.bfloat16),
        jnp.zeros((head_count, seq_len), jnp.float32),
    )
    return lax.fori_loop(0, block_count, query_step, initial)


def attend_back(
    queries, keys_all, values_all, results, d_results, log_totals, text_len, video_len, score_scale
):
    seq_len, head_count, head_dim = queries.shape
    block_count = (TXT + video_len + BLOCK - 1) // BLOCK
    row_dots_all = jnp.einsum("qhd,qhd->hq", d_results, results, preferred_element_type=jnp.float32)

    def query_step(query_block, gradients):
        grad_q, grad_k, grad_v = gradients
        offset = query_block * BLOCK
        query_rows = lax.dynamic_slice_in_dim(queries, offset, BLOCK, 0)
        d_rows = lax.dynamic_slice_in_dim(d_results, offset, BLOCK, 0)
        query_ok = allowed_rows(offset, BLOCK, text_len, video_len)
        log_total = lax.dynamic_slice_in_dim(log_totals, offset, BLOCK, 1)
        row_dots = lax.dynamic_slice_in_dim(row_dots_all, offset, BLOCK, 1)

        def key_step(key_block, inner_state):
            q_sums, grad_k, grad_v = inner_state
            key_offset = key_block * BLOCK
            key_rows = lax.dynamic_slice_in_dim(keys_all, key_offset, BLOCK, 0)
            value_rows = lax.dynamic_slice_in_dim(values_all, key_offset, BLOCK, 0)
            key_ok = allowed_rows(key_offset, BLOCK, text_len, video_len)
            scores, live_pairs = block_scores(query_rows, key_rows, query_ok, key_ok, score_scale)
            probabilities = jnp.exp(jnp.where(live_pairs, scores - log_total[..., None], NEGATIVE))
            probs_low = probabilities.astype(jnp.bfloat16)
            d_probs = jnp.einsum(
                "qhd,khd->hqk", d_rows, value_rows, preferred_element_type=jnp.float32
            )
            d_scores = (probabilities * (d_probs - row_dots[..., None])).astype(jnp.bfloat16)
            q_sums = q_sums + jnp.einsum(
                "hqk,khd->qhd", d_scores, key_rows, preferred_element_type=jnp.float32
            )
            k_part = jnp.einsum(
                "hqk,qhd->khd", d_scores, query_rows, preferred_element_type=jnp.float32
            )
            v_part = jnp.einsum(
                "hqk,qhd->khd", probs_low, d_rows, preferred_element_type=jnp.float32
            )
            grad_k = lax.dynamic_update_slice_in_dim(
                grad_k,
                lax.dynamic_slice_in_dim(grad_k, key_offset, BLOCK, 0) + k_part,
                key_offset,
                0,
            )
            grad_v = lax.dynamic_update_slice_in_dim(
                grad_v,
                lax.dynamic_slice_in_dim(grad_v, key_offset, BLOCK, 0) + v_part,
                key_offset,
                0,
            )
            return (q_sums, grad_k, grad_v)

        q_start = jnp.zeros((BLOCK, head_count, head_dim), jnp.float32)
        q_sums, grad_k, grad_v = lax.fori_loop(0, block_count, key_step, (q_start, grad_k, grad_v))
        grad_q = lax.dynamic_update_slice_in_dim(grad_q, q_sums, offset, 0)
        return (grad_q, grad_k, grad_v)

    zero_grad = jnp.zeros((seq_len, head_count, head_dim), jnp.float32)
    grad_q, grad_k, grad_v = lax.fori_loop(
        0, block_count, query_step, (zero_grad, zero_grad, zero_grad)
    )
    return (
        (grad_q * score_scale).astype(jnp.bfloat16),
        (grad_k * score_scale).astype(jnp.bfloat16),
        grad_v.astype(jnp.bfloat16),
    )


def body(qkv, gate, cotangent, out_weight, clip_lengths, text_lengths, plan):
    groups = lax.axis_size("dp")
    seq_ways = lax.axis_size("seq")
    group_index = lax.axis_index("dp")
    ordinal = jnp.arange(groups, dtype=jnp.int32)
    inverse = jnp.sum(jnp.where(plan[None, :] == ordinal[:, None], ordinal[None, :], 0), axis=1)
    home_clip = 2 * group_index
    head_width = out_weight.shape[0]
    local_width = head_width // seq_ways
    head_count = local_width // HD
    row_count = cotangent.shape[1]
    score_scale = HD ** (-0.5)
    clip_ids = (home_clip, home_clip + 1)
    spread_heads = to_heads(qkv, seq_ways)
    seq_len = spread_heads.shape[1]
    video_lens = [clip_lengths[clip_id] for clip_id in clip_ids]
    text_lens = [text_lengths[clip_id] for clip_id in clip_ids]
    sections = []
    result_list = []
    log_list = []
    for slot_index in range(2):
        triple = [
            spread_heads[slot_index, :, member].reshape(seq_len, head_count, HD)
            for member in range(3)
        ]
        results, log_totals = attend(
            triple[0],
            triple[1],
            triple[2],
            text_lens[slot_index],
            video_lens[slot_index],
            score_scale,
        )
        sections.append(triple)
        result_list.append(results)
        log_list.append(log_totals)
    attn_heads = jnp.stack(result_list).reshape(2, seq_len, 1, local_width)
    attn_back = lax.all_to_all(attn_heads, "seq", split_axis=1, concat_axis=2, tiled=True).reshape(
        2, row_count, head_width
    )
    attn_here = jnp.stack([attn_back[0], move_in(attn_back[1], inverse)])
    outputs = jnp.einsum("crh,hd->crd", attn_here, out_weight, preferred_element_type=jnp.float32)
    mixed = (gate[:, None, :] * outputs).astype(jnp.bfloat16)
    gate_grad = lax.psum(jnp.sum(cotangent.astype(jnp.float32) * outputs, axis=1), "seq")
    scaled = (cotangent.astype(jnp.float32) * gate[:, None, :]).astype(jnp.bfloat16)
    partial_weight = jnp.einsum(
        "crh,crd->hd", attn_here, scaled, preferred_element_type=jnp.float32
    )
    weight_grad = lax.psum_scatter(partial_weight, ("dp", "seq"), scatter_dimension=1, tiled=True)
    d_attn = jnp.einsum(
        "crd,hd->crh", scaled, out_weight, preferred_element_type=jnp.float32
    ).astype(jnp.bfloat16)
    d_attn = jnp.stack([d_attn[0], move_out(d_attn[1], plan)])
    d_parted = d_attn.reshape(2, row_count, seq_ways, local_width)
    d_heads = lax.all_to_all(d_parted, "seq", split_axis=2, concat_axis=1, tiled=True).reshape(
        2, seq_len, local_width
    )
    grad_list = []
    for slot_index in range(2):
        triple = sections[slot_index]
        d_rows = d_heads[slot_index].reshape(seq_len, head_count, HD)
        grad_parts = attend_back(
            triple[0],
            triple[1],
            triple[2],
            result_list[slot_index],
            d_rows,
            log_list[slot_index],
            text_lens[slot_index],
            video_lens[slot_index],
            score_scale,
        )
        grad_list.append(
            jnp.stack([grad_part.reshape(seq_len, local_width) for grad_part in grad_parts], axis=1)
        )
    grad_heads = jnp.stack(grad_list).reshape(2, seq_len, 3, 1, local_width)
    grad_tokens = lax.all_to_all(
        grad_heads, "seq", split_axis=1, concat_axis=3, tiled=True
    ).reshape(2, row_count, 3 * head_width)
    return (mixed, gate_grad, weight_grad, grad_tokens)


def solution(mesh):
    in_specs = (P("dp", "seq", None), P("dp", None), P("dp", "seq", None), P(), P(), P(), P())
    out_specs = (P("dp", "seq", None), P("dp", None), P(None, ("dp", "seq")), P("dp", "seq", None))
    return jax.shard_map(body, mesh=mesh, in_specs=in_specs, out_specs=out_specs, check_vma=False)
```

profile of v0, /device:TPU:0, one launch (start us, length us, event | category | flops | bytes accessed | tf_op | source)
XLA Modules:
  0.0 685.4 jit_solution(15240919049325818665)
XLA Ops:
  7.2 9.5 %fusion.170 = bf16[2,256,1536]{2,1,0:T(8,128)(2,1)S(1)} fusion(bf16[1536,3072]{1,0:T(8,128)(2,1)} %param.32, bf16[2,256,3072]{2,1,0:T(8,128)(2,1)} %param.31, f32[2,3072]{1,0:T(2,128)} %param.30), kind=kOutput, calls=%fused_computation.205 | convolution fusion | flops 4837343232 | bytes 14180352 | tf_op jit(solution)/shard_map/crd,hd->crh/dot_general | solution.py:228
  17.9 5.2 all-to-all-start.4
  23.1 6.6 copy.215
  29.7 5.0 copy.216
  35.7 5.0 all-to-all-start
  45.6 99.6 %all-to-all-done = bf16[2,256,3,4,384]{1,4,2,0,3:T(8,128)(2,1)} async-done(((bf16[2,256,3,4,384]{1,4,2,0,3:T(8,128)(2,1)}), bf16[2,256,3,4,384]{1,4,2,0,3:T(8,128)(2,1)}, u32[]{:S(2)}, u32[]{:S(2)}) %all-to-all-start) | async-done | bytes 4718624 | tf_op jit(solution)/shard_map/all_to_all | solution.py:39
  145.2 4.2 all-to-all-start.5
  149.4 6.6 copy.217
  156.1 4.0 fusion.179
  164.1 7.3 %while.232 = (s32[]{:T(128)}, bf16[1024,3,128]{0,2,1:T(8,128)(2,1)S(1)}, f32[3,1024]{1,0:T(4,128)}, s32[]{:T(128)}, bf16[1024,3,128]{2,0,1:T(8,128)(2,1)}, /*ind...) while((s32[]{:T(128)}, ...), condition=%wide.region_7.8_spmd, body=%wide.region_0.7_spmd.sunk | while | flops 613564928 | bytes 14026621 | solution.py:108
  168.1 3.2 while.241
  168.9 2.4 fusion.296
  171.4 2.6 copy.223
  174.0 2.3 copy.226
  179.0 2.3 copy.225
  182.9 8.6 %while.235 = (s32[]{:T(128)}, bf16[1024,3,128]{0,2,1:T(8,128)(2,1)}, f32[3,1024]{1,0:T(4,128)}, s32[]{:T(128)}, bf16[1024,3,128]{2,0,1:T(8,128)(2,1)}, /*index=5...) while((s32[]{:T(128)}, bf16[1024,3,128]{0,2,1:T(8,128)(2,1)}, ...), condition=%wide.region_15.16_spmd, body=%wide.region_8.15_spmd.sunk | while | flops 613564928 | bytes 14026621 | solution.py:108
  184.4 2.4 while.242
  187.5 3.2 while.243
  188.4 2.4 fusion.288
  193.4 2.9 copy.228
  196.3 3.7 all-to-all-start.1
  202.8 2.3 pad_maximum_fusion.2
  206.5 15.0 %all-to-all-done.1 = bf16[2,1024,1,384]{3,0,2,1:T(2,128)(2,1)S(1)} async-done(((bf16[2,1024,1,384]{3,0,2,1:T(2,128)(2,1)}), bf16[2,1024,1,384]{3,0,2,1:T(2,128)(2,1)S(1)}, u32[]{:S(2)}, u32[]{:S(2)}) %all-to-all-start.1) | async-done | bytes 1572896 | tf_op jit(solution)/shard_map/all_to_all | solution.py:216
  222.6 3.6 all-to-all-start.6
  230.8 28.5 %all-to-all-done.6 = bf16[2,256,4,384]{3,1,0,2:T(8,128)(2,1)S(1)} async-done(((bf16[2,256,4,384]{3,1,0,2:T(8,128)(2,1)}), bf16[2,256,4,384]{3,1,0,2:T(8,128)(2,1)S(1)}, u32[]{:S(2)}, u32[]{:S(2)}) %all-to-all-start.6) | async-done | bytes 1572896 | tf_op jit(solution)/shard_map/all_to_all | solution.py:233
  259.3 60.3 %all-to-all-start.2 = ((bf16[8,32,1536]{2,1,0:T(8,128)(2,1)}), bf16[8,32,1536]{2,1,0:T(8,128)(2,1)S(1)}, u32[]{:S(2)}, u32[]{:S(2)}) async-start(bf16[8,32,1536]{2,1,0:T(8,128)(2,1)} %reshape_squeeze.36), calls=%async_computation.2 | async-start | bytes 1572864 | tf_op jit(solution)/shard_map/all_to_all | solution.py:20
  323.2 2.6 reshape_squeeze.38
  328.0 2.5 reshape_squeeze.39
  335.4 4.2 all-to-all-start.3
  342.4 11.7 %while.237 = (s32[]{:T(128)}, f32[1024,3,128]{0,2,1:T(8,128)}, f32[1024,3,128]{2,0,1:T(8,128)S(1)}, f32[1024,3,128]{2,0,1:T(8,128)}, s32[]{:T(128)}, /*index=5*/...) while((s32[]{:T(128)}, f32[1024,3,128]{0,2,1:T(8,128)}, ...), condition=%wide.region_23.25_spmd, body=%wide.region_20.24_spmd.sunk | while | flops 1015355392 | bytes 31900368 | solution.py:169
  346.3 6.7 while.244
  350.0 3.0 fusion.280
  354.1 2.9 copy.249
  360.1 11.0 %convolution_bitcast_fusion.4 = f32[1536,3072]{0,1:T(8,128)} fusion(bf16[2,256,3072]{2,1,0:T(8,128)(2,1)} %param.31, f32[2,3072]{1,0:T(2,128)S(1)} %copy-done.26, bf16[1,256,1536]{2,1,0:T(8,128)(2,1)} %bitcast.27, bf16[1,256,1536]{2,1,0:T(8,128)(2,1)S(1)} %slice.49), kind=kOutput, calls=%fused_computation.194 | convolution fusion | flops 4837343232 | bytes 23617536 | tf_op jit(solution)/shard_map/crh,crd->hd/dot_general | solution.py:224
  375.1 12.7 %while.239 = (s32[]{:T(128)}, f32[1024,3,128]{0,2,1:T(8,128)}, f32[1024,3,128]{2,0,1:T(8,128)}, f32[1024,3,128]{2,0,1:T(8,128)}, s32[]{:T(128)}, /*index=5*/bf16...) while((s32[]{:T(128)}, f32[1024,3,128]{0,2,1:T(8,128)}, ...), condition=%wide.region_27.29_spmd, body=%wide.region_24.28_spmd.sunk | while | flops 1015355392 | bytes 44483340 | solution.py:169
  379.2 7.7 %while.245 = (s32[]{:T(128)}, f32[512,3,128]{0,2,1:T(8,128)S(1)}, f32[1024,3,128]{2,0,1:T(8,128)}, f32[1024,3,128]{2,0,1:T(8,128)}, s32[]{:T(128)}, /*index=5*/b...) while((s32[]{:T(128)}, f32[512,3,128]{0,2,1:T(8,128)S(1)}, ...), condition=%wide.region_26.27_spmd.clone.clone, body=%wide.region_25.26_spmd.clone.clone.sunk | while | flops 1015355392 | bytes 39739748 | solution.py:164
  383.9 3.0 fusion.264
  389.5 2.7 copy.242
  392.7 2.7 copy.251
  399.1 2.6 maximum_bitcast_fusion
  401.7 12.8 %copy.252 = bf16[2,1024,3,1,384]{4,0,3,2,1:T(2,128)(2,1)} copy(bf16[2,1024,3,1,384]{1,4,2,0,3:T(8,128)(2,1)} %maximum_bitcast_fusion) | data formatting | bytes 9437184 | tf_op jit(solution)/shard_map/reshape | solution.py:254
  414.5 5.2 all-to-all-start.7
  419.7 10.1 %fusion.168 = (f32[2,3072]{1,0:T(2,128)S(1)}, bf16[2,256,3072]{2,1,0:T(8,128)(2,1)}) fusion(bf16[2,256,3072]{2,1,0:T(8,128)(2,1)} %param.31, f32[2,3072]{1,0:T(2,128)S(1)} %copy-done.27, bf16[1536,3072]{1,0:T(8,128)(2,1)} %param.32, bf16[1,256,1536]{2,1,0:T(8,128)(2,1)} %bitcast.27, bf16[1,256,1536]{2,1,0:T(8,128)(2,1)S(1)} %copy-done.21), kind=kOutput, calls=%fused_computation.201 | convolution fusion | flops 4840482816 | bytes 17350656 | tf_op jit(solution)/shard_map/crh,hd->crd/dot_general | solution.py:220
  429.8 139.7 %psum.7 = f32[2,3072]{1,0:T(2,128)} all-reduce(f32[2,3072]{1,0:T(2,128)S(1)} %get-tuple-element.2791), channel_id=1, replica_groups=mesh['dp'=8,'seq'=4] {'seq'}, use_global_device_ids=true, to_apply=%region_18.20 | all-reduce | flops 6144 | bytes 49152 | tf_op jit(solution)/shard_map/psum | solution.py:222
  569.6 5.2 copy.253
  574.8 6.7 copy.254
  581.5 6.6 copy.255
  588.1 90.2 %reduce-scatter.2.cloned.1.call-done = f32[1536,96]{0,1:T(8,128)} async-done(((f32[1536,3072]{0,1:T(8,128)}), f32[1536,96]{0,1:T(8,128)}) %reduce-scatter.2.cloned.1.call-update) | async-done | bytes 589840 | tf_op jit(solution)/shard_map/reduce_scatter | solution.py:227
  (176 shorter events, 81.1 us)
Async XLA Ops:
  17.9 17.8 %all-to-all-start.4 = ((bf16[8,32,1536]{2,1,0:T(8,128)(2,1)}), bf16[8,32,1536]{2,1,0:T(8,128)(2,1)S(1)}, u32[]{:S(2)}, u32[]{:S(2)}) async-start(bf16[8,32,1536]{2,1,0:T(8,128)(2,1)} %bitcast.30), calls=%async_computation.5 | async-start | bytes 1572864 | tf_op jit(solution)/shard_map/all_to_all | solution.py:29
  34.7 6.0 copy-start.24
  34.7 6.0 copy-start.25
  34.7 9.2 %copy-start.28 = (s32[8]{0:T(128)S(1)}, s32[8]{0:T(128)}, u32[]{:S(2)}) copy-start(s32[8]{0:T(128)} %param.35) | copy-start | bytes 100
  35.7 109.5 %all-to-all-start = ((bf16[2,256,3,4,384]{1,4,2,0,3:T(8,128)(2,1)}), bf16[2,256,3,4,384]{1,4,2,0,3:T(8,128)(2,1)}, u32[]{:S(2)}, u32[]{:S(2)}) async-start(bf16[2,256,3,4,384]{1,4,2,0,3:T(8,128)(2,1)} %copy.216), calls=%async_computation | async-start | bytes 9437184 | tf_op jit(solution)/shard_map/all_to_all | solution.py:39
  145.2 51.0 %all-to-all-start.5 = ((bf16[8,32,1536]{2,1,0:T(8,128)(2,1)}), bf16[8,32,1536]{2,1,0:T(8,128)(2,1)}, u32[]{:S(2)}, u32[]{:S(2)}) async-start(bf16[8,32,1536]{2,1,0:T(8,128)(2,1)} %broadcast_select_fusion), calls=%async_computation.6 | async-start | bytes 1572864 | tf_op jit(solution)/shard_map/all_to_all | solution.py:31
  171.4 7.6 %copy-start.9 = (bf16[1024,3,128]{0,2,1:T(8,128)(2,1)}, bf16[1024,3,128]{0,2,1:T(8,128)(2,1)S(1)}, u32[]{:S(2)}) copy-start(bf16[1024,3,128]{0,2,1:T(8,128)(2,1)S(1)} %get-tuple-element.1855) | copy-start | bytes 2359300
  171.4 4.9 copy-start.14
  191.6 4.7 copy-start
  196.3 3.7 copy-start.18
  196.3 25.2 %all-to-all-start.1 = ((bf16[2,1024,1,384]{3,0,2,1:T(2,128)(2,1)}), bf16[2,1024,1,384]{3,0,2,1:T(2,128)(2,1)S(1)}, u32[]{:S(2)}, u32[]{:S(2)}) async-start(bf16[2,1024,1,384]{3,0,2,1:T(2,128)(2,1)} %copy.228), calls=%async_computation.1 | async-start | bytes 3145728 | tf_op jit(solution)/shard_map/all_to_all | solution.py:216
  205.1 21.1 %copy-start.29 = (s32[8]{0:T(128)S(1)}, s32[8]{0:T(128)}, u32[]{:S(2)}) copy-start(s32[8]{0:T(128)} %param.35) | copy-start | bytes 100
  221.5 1.1 copy-start.11
  222.6 36.7 %all-to-all-start.6 = ((bf16[2,256,4,384]{3,1,0,2:T(8,128)(2,1)}), bf16[2,256,4,384]{3,1,0,2:T(8,128)(2,1)S(1)}, u32[]{:S(2)}, u32[]{:S(2)}) async-start(bf16[2,256,4,384]{3,1,0,2:T(8,128)(2,1)} %copy.233), calls=%async_computation.7 | async-start | bytes 3145728 | tf_op jit(solution)/shard_map/all_to_all | solution.py:233
  259.3 74.4 %all-to-all-start.2 = ((bf16[8,32,1536]{2,1,0:T(8,128)(2,1)}), bf16[8,32,1536]{2,1,0:T(8,128)(2,1)S(1)}, u32[]{:S(2)}, u32[]{:S(2)}) async-start(bf16[8,32,1536]{2,1,0:T(8,128)(2,1)} %reshape_squeeze.36), calls=%async_computation.2 | async-start | bytes 1572864 | tf_op jit(solution)/shard_map/all_to_all | solution.py:20
  321.0 9.6 %copy-start.15 = (bf16[1024,3,128]{0,2,1:T(8,128)(2,1)S(1)}, bf16[1024,3,128]{0,2,1:T(8,128)(2,1)}, u32[]{:S(2)}) copy-start(bf16[1024,3,128]{0,2,1:T(8,128)(2,1)} %get-tuple-element.4286) | copy-start | bytes 2359300
  323.2 8.5 %copy-start.10 = (bf16[1024,3,128]{0,2,1:T(8,128)(2,1)S(1)}, bf16[1024,3,128]{0,2,1:T(8,128)(2,1)}, u32[]{:S(2)}) copy-start(bf16[1024,3,128]{0,2,1:T(8,128)(2,1)} %copy-done.9) | copy-start | bytes 2359300
  335.4 24.8 %all-to-all-start.3 = ((bf16[8,32,1536]{2,1,0:T(8,128)(2,1)}), bf16[8,32,1536]{2,1,0:T(8,128)(2,1)}, u32[]{:S(2)}, u32[]{:S(2)}) async-start(bf16[8,32,1536]{2,1,0:T(8,128)(2,1)} %broadcast_select_fusion.1), calls=%async_computation.3 | async-start | bytes 1572864 | tf_op jit(solution)/shard_map/all_to_all | solution.py:22
  339.6 338.7 %reduce-scatter.2.cloned.1.call-start = ((), (), s32[]{:S(2)}) async-start(), calls=%async_computation.9 | async-start | bytes 19464192 | tf_op jit(solution)/shard_map/reduce_scatter | solution.py:227
  346.4 1.4 copy-start.7
  346.4 1.4 copy-start.23
  354.0 6.1 copy-start.2
  354.1 5.1 copy-start.19
  354.1 6.1 copy-start.26
  360.1 11.0 %copy-start.20 = (bf16[1,256,1536]{2,1,0:T(8,128)(2,1)}, bf16[1,256,1536]{2,1,0:T(8,128)(2,1)S(1)}, u32[]{:S(2)}) copy-start(bf16[1,256,1536]{2,1,0:T(8,128)(2,1)S(1)} %slice.49) | copy-start | bytes 2359300
  371.2 3.9 copy-start.1
  375.1 12.8 %copy-start.3 = (f32[1024,3,128]{2,0,1:T(8,128)S(1)}, f32[1024,3,128]{2,0,1:T(8,128)}, u32[]{:S(2)}) copy-start(f32[1024,3,128]{2,0,1:T(8,128)} %copy-done.2) | copy-start | bytes 4718596
  379.3 1.4 copy-start.8
  379.3 1.4 copy-start.22
  380.7 1.4 copy-start.4
  382.8 1.1 copy-start.5
  389.5 2.7 copy-start.6
  392.7 4.3 copy-start.12
  395.4 1.8 copy-start.17
  397.2 1.4 copy-start.13
  397.4 1.4 copy-start.16
  414.5 5.2 copy-start.21
  414.5 5.2 copy-start.27
  414.5 155.0 %all-to-all-start.7 = ((bf16[2,1024,3,1,384]{4,0,3,2,1:T(2,128)(2,1)}), bf16[2,1024,3,1,384]{4,0,3,2,1:T(2,128)(2,1)}, u32[]{:S(2)}, u32[]{:S(2)}) async-start(bf16[2,1024,3,1,384]{4,0,3,2,1:T(2,128)(2,1)} %copy.252), calls=%async_computation.8 | async-start | bytes 9437184 | tf_op jit(solution)/shard_map/all_to_all | solution.py:255
Sparse Core Ops, SparseCore 0:
  371.3 306.9 reduce-scatter.1
where the time goes:
time: 697 us; the launch traced here: 685 us
  waiting for transfers between devices  234 us (34%)
  blocking collectives  140 us (20%)
  local copies, waits for them, and re-layouts  129 us (19%)
  starting transfers between devices  91.4 us (13%)
  matrix products  48.5 us (7%)
  other arithmetic  24.1 us (3%)
  between operations  17.3 us (2%)
    psum x1, blocking collectives, body(): lax.psum(jnp.sum(cotangent.astype(jnp.float32) * outputs, axis=1), 'seq')  140 us
    all_to_all x1, waiting for transfers between devices, to_heads(): lax.all_to_all(parted, 'seq', split_axis=3, concat_axis=1, tiled=True)  99.6 us
    reduce_scatter x1, waiting for transfers between devices, body(): lax.psum_scatter(partial_weight, ('dp', 'seq'), scatter_dimension=1, tile...  90.2 us
    all_to_all x1, starting transfers between devices, move_in(): lax.all_to_all(portions, 'dp', split_axis=0, concat_axis=0, tiled=True)  60.3 us
    all_to_all x1, waiting for transfers between devices, body(): lax.all_to_all(d_parted, 'seq', split_axis=2, concat_axis=1, tiled=True)  28.5 us
    unnamed x50, local copies, waits for them, and re-layouts  15.6 us
    all_to_all x1, waiting for transfers between devices, body(): lax.all_to_all(attn_heads, 'seq', split_axis=1, concat_axis=2, tiled=True)  15 us
  transfers between devices with their start and end apart: 9, of which 5 were waited for; matrix products, arithmetic and copies ran while one was open for 25% of the time, Pallas kernels for 0%

commit v1 on v0

--- a/solution.py
+++ b/solution.py
@@ -9,6 +9,30 @@
 NEGATIVE = -1e30
 
 
+def cut_along(x, dim, size):
+    dims = x.shape
+    parts = x.reshape(*dims[:dim], size, dims[dim] // size, *dims[dim + 1 :])
+    return jnp.moveaxis(parts, dim, 0)
+
+
+def laid_out(blocks, dim):
+    lengths = list(blocks.shape[1:])
+    lengths[dim] *= blocks.shape[0]
+    return jnp.moveaxis(blocks, 0, dim).reshape(lengths)
+
+
+def exchange_directly(x, axis, split_dim, concat_dim):
+    devices, index = (lax.axis_size(axis), lax.axis_index(axis))
+    blocks = cut_along(x, split_dim, devices)
+    out = blocks
+    for step in range(1, devices):
+        target, source = ((index + step) % devices, (index - step) % devices)
+        sent = lax.dynamic_index_in_dim(blocks, target, 0)
+        received = lax.ppermute(sent, axis, [(i, (i + step) % devices) for i in range(devices)])
+        out = lax.dynamic_update_slice_in_dim(out, received, source, axis=0)
+    return laid_out(out, concat_dim)
+
+
 def allowed_rows(offset, count, text_len, video_len):
     places = offset + jnp.arange(count, dtype=jnp.int32)
     return (places < text_len) | (places >= TXT) & (places < TXT + video_len)
@@ -17,7 +41,7 @@
 def move_in(block_rows, inverse):
     groups = lax.axis_size("dp")
     portions = block_rows.reshape(groups, block_rows.shape[0] // groups, block_rows.shape[1])
-    spread = lax.all_to_all(portions, "dp", split_axis=0, concat_axis=0, tiled=True)
+    spread = exchange_directly(portions, "dp", 0, 0)
     arranged = jnp.take(spread, inverse, axis=0)
     landed = lax.all_to_all(arranged, "dp", split_axis=0, concat_axis=0, tiled=True)
     return landed.reshape(block_rows.shape)

time: 697 us -> 675 us (0.968)
  waiting for transfers between devices: 234 us -> 213 us
    ppermute x0 -> x7, starting transfers between devices: none -> 61.3 us  [exchange_directly(): lax.ppermute(sent, axis, [(i, (i + step) % devices) for i in range(device...]
    all_to_all x1 -> x0, starting transfers between devices: 60.3 us -> none  [move_in(): lax.all_to_all(portions, 'dp', split_axis=0, concat_axis=0, tiled=True)]
    all_to_all x1, waiting for transfers between devices: 28.5 us -> 0.01 us  [body(): lax.all_to_all(d_parted, 'seq', split_axis=2, concat_axis=1, tiled=True)]
    all_to_all x1, waiting for transfers between devices: 0.98 us -> 12.5 us  [move_out(): lax.all_to_all(portions, 'dp', split_axis=0, concat_axis=0, tiled=True)]
    all_to_all x1, waiting for transfers between devices: 15 us -> 7.9 us  [body(): lax.all_to_all(attn_heads, 'seq', split_axis=1, concat_axis=2, tiled=True)]
    unnamed x50 -> x48, local copies, waits for them, and re-layouts: 15.6 us -> 14.8 us
  transfers between devices with their start and end apart: 9 -> 15, of which waited for: 5 -> 8; matrix products, arithmetic and copies ran while one was open for 25% -> 25% of each run, Pallas kernels for 0% -> 0%
where the time goes in v1:
time: 675 us; the launch traced here: 663 us
  waiting for transfers between devices  213 us (32%)
  blocking collectives  140 us (21%)
  local copies, waits for them, and re-layouts  125 us (19%)
  starting transfers between devices  95.1 us (14%)
  matrix products  48.5 us (7%)
  other arithmetic  23.1 us (3%)
  between operations  17.4 us (3%)
    psum x1, blocking collectives, body(): lax.psum(jnp.sum(cotangent.astype(jnp.float32) * outputs, axis=1), 'seq')  140 us
    all_to_all x1, waiting for transfers between devices, to_heads(): lax.all_to_all(parted, 'seq', split_axis=3, concat_axis=1, tiled=True)  98.3 us
    reduce_scatter x1, waiting for transfers between devices, body(): lax.psum_scatter(partial_weight, ('dp', 'seq'), scatter_dimension=1, tile...  91.1 us
    ppermute x7, starting transfers between devices, exchange_directly(): lax.ppermute(sent, axis, [(i, (i + step) % devices) for i in range(device...  61.3 us
    unnamed x48, local copies, waits for them, and re-layouts  14.8 us
  transfers between devices with their start and end apart: 15, of which 8 were waited for; matrix products, arithmetic and copies ran while one was open for 25% of the time, Pallas kernels for 0%

profile of v1, /device:TPU:0, one launch (start us, length us, event | category | flops | bytes accessed | tf_op | source)
XLA Modules:
  0.0 663.0 jit_solution(13473305619400053180)
XLA Ops:
  7.2 9.5 %fusion.170 = bf16[2,256,1536]{2,1,0:T(8,128)(2,1)S(1)} fusion(bf16[1536,3072]{1,0:T(8,128)(2,1)} %param.32, bf16[2,256,3072]{2,1,0:T(8,128)(2,1)} %param.31, f32[2,3072]{1,0:T(2,128)} %param.30), kind=kOutput, calls=%fused_computation.205 | convolution fusion | flops 4837343232 | bytes 14180352 | tf_op jit(solution)/shard_map/crd,hd->crh/dot_general | solution.py:252
  17.7 5.2 all-to-all-start.3
  22.9 12.5 %all-to-all-done.3 = bf16[8,32,1536]{2,1,0:T(8,128)(2,1)S(1)} async-done(((bf16[8,32,1536]{2,1,0:T(8,128)(2,1)}), bf16[8,32,1536]{2,1,0:T(8,128)(2,1)S(1)}, u32[]{:S(2)}, u32[]{:S(2)}) %all-to-all-start.3) | async-done | bytes 786464 | tf_op jit(solution)/shard_map/all_to_all | solution.py:53
  37.1 3.5 all-to-all-start.4
  40.6 6.6 copy.239
  47.2 5.0 copy.240
  53.1 5.0 all-to-all-start
  64.3 98.3 %all-to-all-done = bf16[2,256,3,4,384]{1,4,2,0,3:T(8,128)(2,1)} async-done(((bf16[2,256,3,4,384]{1,4,2,0,3:T(8,128)(2,1)}), bf16[2,256,3,4,384]{1,4,2,0,3:T(8,128)(2,1)}, u32[]{:S(2)}, u32[]{:S(2)}) %all-to-all-start) | async-done | bytes 4718624 | tf_op jit(solution)/shard_map/all_to_all | solution.py:63
  162.6 4.4 all-to-all-start.5
  167.0 6.6 %copy.241 = bf16[2,256,3,4,384]{4,1,3,2,0:T(8,128)(2,1)} copy(bf16[2,256,3,4,384]{1,4,2,0,3:T(8,128)(2,1)} %all-to-all-done) | data formatting | bytes 9437184 | tf_op jit(solution)/shard_map/all_to_all | solution.py:63
  173.6 4.0 fusion.179
  181.7 8.0 %while.232 = (s32[]{:T(128)}, bf16[1024,3,128]{0,2,1:T(8,128)(2,1)S(1)}, f32[3,1024]{1,0:T(4,128)}, s32[]{:T(128)}, bf16[1024,3,128]{2,0,1:T(8,128)(2,1)}, /*ind...) while((s32[]{:T(128)}, ...), condition=%wide.region_7.8_spmd, body=%wide.region_0.7_spmd.sunk | while | flops 613564928 | bytes 14026621 | solution.py:132
  182.8 2.4 while.240
  185.9 3.3 while.241
  186.8 2.4 fusion.296
  189.7 2.6 copy.247
  197.3 2.3 copy.249
  201.2 8.1 %while.235 = (s32[]{:T(128)}, bf16[1024,3,128]{0,2,1:T(8,128)(2,1)}, f32[3,1024]{1,0:T(4,128)}, s32[]{:T(128)}, bf16[1024,3,128]{2,0,1:T(8,128)(2,1)}, /*index=5...) while((s32[]{:T(128)}, bf16[1024,3,128]{0,2,1:T(8,128)(2,1)}, ...), condition=%wide.region_15.16_spmd, body=%wide.region_8.15_spmd.sunk | while | flops 613564928 | bytes 14026621 | solution.py:132
  202.3 2.3 while.242
  205.3 3.2 while.243
  206.2 2.4 fusion.288
  211.2 2.9 copy.252
  214.1 5.0 all-to-all-start.1
  219.3 2.7 fusion.180
  224.3 2.5 reshape_squeeze.34
  229.0 2.5 reshape_squeeze.35
  232.7 7.9 %all-to-all-done.1 = bf16[2,1024,1,384]{3,0,2,1:T(2,128)(2,1)S(1)} async-done(((bf16[2,1024,1,384]{3,0,2,1:T(2,128)(2,1)}), bf16[2,1024,1,384]{3,0,2,1:T(2,128)(2,1)S(1)}, u32[]{:S(2)}, u32[]{:S(2)}) %all-to-all-start.1) | async-done | bytes 1572896 | tf_op jit(solution)/shard_map/all_to_all | solution.py:240
  243.6 35.6 %collective-permute-start = (bf16[1,1,32,1536]{3,2,1,0:T(8,128)(2,1)}, bf16[1,1,32,1536]{3,2,1,0:T(8,128)(2,1)S(1)}, u32[]{:S(2)}, u32[]{:S(2)}) collective-permute-start(bf16[1,1,32,1536]{3,2,1,0:T(8,128)(2,1)} %get-tuple-element.2811), channel_id=1, source_target_pairs={{0,4},{4,8},{8,12},{12,16},{16,20},{20,24},{24,28},{28,0},{1,5},{5... | collective-permute-start | bytes 294920 | tf_op jit(solution)/shard_map/ppermute | solution.py:31
  281.6 20.1 %collective-permute-start.2 = (bf16[1,1,32,1536]{3,2,1,0:T(8,128)(2,1)S(1)}, bf16[1,1,32,1536]{3,2,1,0:T(8,128)(2,1)S(1)}, u32[]{:S(2)}, u32[]{:S(2)}) collective-permute-start(bf16[1,1,32,1536]{3,2,1,0:T(8,128)(2,1)S(1)} %copy-done.21), channel_id=1, source_target_pairs={{0,12},{4,16},{8,20},{12,24},{16,28},{20,0},{24,4},{28,8},{1,13},{... | collective-permute-start | bytes 294920 | tf_op jit(solution)/shard_map/ppermute | solution.py:31
  304.9 2.4 collective-permute-start.6
  311.1 5.4 all-to-all-start.2
  319.4 11.8 %while.237 = (s32[]{:T(128)}, f32[1024,3,128]{0,2,1:T(8,128)}, f32[1024,3,128]{2,0,1:T(8,128)S(1)}, f32[1024,3,128]{2,0,1:T(8,128)}, s32[]{:T(128)}, /*index=5*/...) while((s32[]{:T(128)}, f32[1024,3,128]{0,2,1:T(8,128)}, ...), condition=%wide.region_23.25_spmd, body=%wide.region_20.24_spmd.sunk | while | flops 1015355392 | bytes 31900368 | solution.py:193
  323.3 6.9 %while.244 = (s32[]{:T(128)}, f32[512,3,128]{0,2,1:T(8,128)S(1)}, f32[1024,3,128]{2,0,1:T(8,128)S(1)}, f32[1024,3,128]{2,0,1:T(8,128)}, s32[]{:T(128)}, /*index=...) while((s32[]{:T(128)}, f32[512,3,128]{0,2,1:T(8,128)S(1)}, ...), condition=%wide.region_22.23_spmd.clone.clone, body=%wide.region_21.22_spmd.clone.clone.sunk | while | flops 1015355392 | bytes 27156784 | solution.py:188
  327.1 3.1 fusion.280
  331.2 2.9 copy.281
  337.3 11.0 %convolution_bitcast_fusion.4 = f32[1536,3072]{0,1:T(8,128)} fusion(bf16[2,256,3072]{2,1,0:T(8,128)(2,1)} %param.31, f32[2,3072]{1,0:T(2,128)S(1)} %copy-done.25, bf16[1,256,1536]{2,1,0:T(8,128)(2,1)} %bitcast.41, bf16[1,256,1536]{2,1,0:T(8,128)(2,1)S(1)} %slice.49), kind=kOutput, calls=%fused_computation.194 | convolution fusion | flops 4837343232 | bytes 23617536 | tf_op jit(solution)/shard_map/crh,crd->hd/dot_general | solution.py:248
  352.2 12.7 %while.239 = (s32[]{:T(128)}, f32[1024,3,128]{0,2,1:T(8,128)}, f32[1024,3,128]{2,0,1:T(8,128)}, f32[1024,3,128]{2,0,1:T(8,128)}, s32[]{:T(128)}, /*index=5*/bf16...) while((s32[]{:T(128)}, f32[1024,3,128]{0,2,1:T(8,128)}, ...), condition=%wide.region_27.29_spmd, body=%wide.region_24.28_spmd.sunk | while | flops 1015355392 | bytes 44483340 | solution.py:193
  356.3 7.7 %while.245 = (s32[]{:T(128)}, f32[512,3,128]{0,2,1:T(8,128)S(1)}, f32[1024,3,128]{2,0,1:T(8,128)}, f32[1024,3,128]{2,0,1:T(8,128)}, s32[]{:T(128)}, /*index=5*/b...) while((s32[]{:T(128)}, f32[512,3,128]{0,2,1:T(8,128)S(1)}, ...), condition=%wide.region_26.27_spmd.clone.clone, body=%wide.region_25.26_spmd.clone.clone.sunk | while | flops 1015355392 | bytes 39739748 | solution.py:188
  361.0 3.0 fusion.264
  375.8 2.6 maximum_bitcast_fusion
  378.4 12.9 %copy.284 = bf16[2,1024,3,1,384]{4,0,3,2,1:T(2,128)(2,1)} copy(bf16[2,1024,3,1,384]{1,4,2,0,3:T(8,128)(2,1)} %maximum_bitcast_fusion) | data formatting | bytes 9437184 | tf_op jit(solution)/shard_map/reshape | solution.py:278
  391.3 5.2 all-to-all-start.6
  396.5 10.1 %fusion.168 = (f32[2,3072]{1,0:T(2,128)S(1)}, bf16[2,256,3072]{2,1,0:T(8,128)(2,1)}) fusion(bf16[2,256,3072]{2,1,0:T(8,128)(2,1)} %param.31, f32[2,3072]{1,0:T(2,128)S(1)} %copy-done.26, bf16[1536,3072]{1,0:T(8,128)(2,1)} %param.32, bf16[1,256,1536]{2,1,0:T(8,128)(2,1)} %bitcast.41, bf16[1,256,1536]{2,1,0:T(8,128)(2,1)S(1)} %copy-done.19), kind=kOutput, calls=%fused_computation.201 | convolution fusion | flops 4840482816 | bytes 17350656 | tf_op jit(solution)/shard_map/crh,hd->crd/dot_general | solution.py:244
  406.6 139.7 %psum.7 = f32[2,3072]{1,0:T(2,128)} all-reduce(f32[2,3072]{1,0:T(2,128)S(1)} %get-tuple-element.2791), channel_id=1, replica_groups=mesh['dp'=8,'seq'=4] {'seq'}, use_global_device_ids=true, to_apply=%region_18.20 | all-reduce | flops 6144 | bytes 49152 | tf_op jit(solution)/shard_map/psum | solution.py:246
  546.3 5.2 copy.285
  551.4 6.7 %copy.286 = bf16[2,256,3,4,1,384]{1,5,3,2,0,4:T(8,128)(2,1)} copy(bf16[2,256,3,4,1,384]{5,1,3,2,0,4:T(8,128)(2,1)} %bitcast.297) | data formatting | bytes 9437184 | tf_op jit(solution)/shard_map/all_to_all | solution.py:279
  558.1 6.6 %copy.287 = bf16[2,256,4608]{2,1,0:T(8,128)(2,1)} copy(bf16[2,256,4608]{1,2,0:T(8,128)(2,1)} %bitcast.298) | data formatting | bytes 9437184
  564.7 91.1 %reduce-scatter.2.cloned.1.call-done = f32[1536,96]{0,1:T(8,128)} async-done(((f32[1536,3072]{0,1:T(8,128)}), f32[1536,96]{0,1:T(8,128)}) %reduce-scatter.2.cloned.1.call-update) | async-done | bytes 589840 | tf_op jit(solution)/shard_map/reduce_scatter | solution.py:251
  (195 shorter events, 86.6 us)
Async XLA Ops:
  16.7 6.2 copy-start.27
  17.7 17.8 %all-to-all-start.3 = ((bf16[8,32,1536]{2,1,0:T(8,128)(2,1)}), bf16[8,32,1536]{2,1,0:T(8,128)(2,1)S(1)}, u32[]{:S(2)}, u32[]{:S(2)}) async-start(bf16[8,32,1536]{2,1,0:T(8,128)(2,1)} %bitcast.44), calls=%async_computation.4 | async-start | bytes 1572864 | tf_op jit(solution)/shard_map/all_to_all | solution.py:53
  37.1 16.1 %all-to-all-start.4 = ((bf16[8,32,1536]{2,1,0:T(8,128)(2,1)}), bf16[8,32,1536]{2,1,0:T(8,128)(2,1)S(1)}, u32[]{:S(2)}, u32[]{:S(2)}) async-start(bf16[8,32,1536]{2,1,0:T(8,128)(2,1)} %broadcast_select_fusion), calls=%async_computation.5 | async-start | bytes 1572864 | tf_op jit(solution)/shard_map/all_to_all | solution.py:55
  52.2 5.9 copy-start.23
  52.2 5.9 copy-start.24
  53.1 109.5 %all-to-all-start = ((bf16[2,256,3,4,384]{1,4,2,0,3:T(8,128)(2,1)}), bf16[2,256,3,4,384]{1,4,2,0,3:T(8,128)(2,1)}, u32[]{:S(2)}, u32[]{:S(2)}) async-start(bf16[2,256,3,4,384]{1,4,2,0,3:T(8,128)(2,1)} %copy.240), calls=%async_computation | async-start | bytes 9437184 | tf_op jit(solution)/shard_map/all_to_all | solution.py:63
  162.6 51.4 %all-to-all-start.5 = ((bf16[2,256,4,384]{3,1,0,2:T(8,128)(2,1)}), bf16[2,256,4,384]{3,1,0,2:T(8,128)(2,1)}, u32[]{:S(2)}, u32[]{:S(2)}) async-start(bf16[2,256,4,384]{3,1,0,2:T(8,128)(2,1)} %copy.265), calls=%async_computation.6 | async-start | bytes 3145728 | tf_op jit(solution)/shard_map/all_to_all | solution.py:257
  189.7 7.6 %copy-start.9 = (bf16[1024,3,128]{0,2,1:T(8,128)(2,1)}, bf16[1024,3,128]{0,2,1:T(8,128)(2,1)S(1)}, u32[]{:S(2)}) copy-start(bf16[1024,3,128]{0,2,1:T(8,128)(2,1)S(1)} %get-tuple-element.1855) | copy-start | bytes 2359300
  189.7 4.9 copy-start.14
  209.4 4.7 copy-start
  211.2 7.9 %copy-start.28 = (s32[8]{0:T(128)S(1)}, s32[8]{0:T(128)}, u32[]{:S(2)}) copy-start(s32[8]{0:T(128)} %param.35) | copy-start | bytes 100
  214.1 26.6 %all-to-all-start.1 = ((bf16[2,1024,1,384]{3,0,2,1:T(2,128)(2,1)}), bf16[2,1024,1,384]{3,0,2,1:T(2,128)(2,1)S(1)}, u32[]{:S(2)}, u32[]{:S(2)}) async-start(bf16[2,1024,1,384]{3,0,2,1:T(2,128)(2,1)} %copy.252), calls=%async_computation.1 | async-start | bytes 3145728 | tf_op jit(solution)/shard_map/all_to_all | solution.py:240
  222.0 9.6 %copy-start.15 = (bf16[1024,3,128]{0,2,1:T(8,128)(2,1)S(1)}, bf16[1024,3,128]{0,2,1:T(8,128)(2,1)}, u32[]{:S(2)}) copy-start(bf16[1024,3,128]{0,2,1:T(8,128)(2,1)} %get-tuple-element.4290) | copy-start | bytes 2359300
  240.8 38.3 %copy-start.10 = (bf16[1024,3,128]{0,2,1:T(8,128)(2,1)S(1)}, bf16[1024,3,128]{0,2,1:T(8,128)(2,1)}, u32[]{:S(2)}) copy-start(bf16[1024,3,128]{0,2,1:T(8,128)(2,1)} %copy-done.9) | copy-start | bytes 2359300
  243.6 37.9 %copy-start.22 = (bf16[1,1,32,1536]{3,2,1,0:T(8,128)(2,1)S(1)}, bf16[1,1,32,1536]{3,2,1,0:T(8,128)(2,1)}, u32[]{:S(2)}) copy-start(bf16[1,1,32,1536]{3,2,1,0:T(8,128)(2,1)} %get-tuple-element.2810) | copy-start | bytes 294916
  243.6 38.0 %copy-start.21 = (bf16[1,1,32,1536]{3,2,1,0:T(8,128)(2,1)S(1)}, bf16[1,1,32,1536]{3,2,1,0:T(8,128)(2,1)}, u32[]{:S(2)}) copy-start(bf16[1,1,32,1536]{3,2,1,0:T(8,128)(2,1)} %get-tuple-element.2809) | copy-start | bytes 294916
  243.6 59.5 %collective-permute-start = (bf16[1,1,32,1536]{3,2,1,0:T(8,128)(2,1)}, bf16[1,1,32,1536]{3,2,1,0:T(8,128)(2,1)S(1)}, u32[]{:S(2)}, u32[]{:S(2)}) collective-permute-start(bf16[1,1,32,1536]{3,2,1,0:T(8,128)(2,1)} %get-tuple-element.2811), channel_id=1, source_target_pairs={{0,4},{4,8},{8,12},{12,16},{16,20},{20,24},{24,28},{28,0},{1,5},{5... | collective-permute-start | bytes 294920 | tf_op jit(solution)/shard_map/ppermute | solution.py:31
  281.5 23.4 %collective-permute-start.1 = (bf16[1,1,32,1536]{3,2,1,0:T(8,128)(2,1)S(1)}, bf16[1,1,32,1536]{3,2,1,0:T(8,128)(2,1)S(1)}, u32[]{:S(2)}, u32[]{:S(2)}) collective-permute-start(bf16[1,1,32,1536]{3,2,1,0:T(8,128)(2,1)S(1)} %copy-done.22), channel_id=1, source_target_pairs={{0,8},{4,12},{8,16},{12,20},{16,24},{20,28},{24,0},{28,4},{1,9},{5... | collective-permute-start | bytes 294920 | tf_op jit(solution)/shard_map/ppermute | solution.py:31
  281.6 25.7 %collective-permute-start.2 = (bf16[1,1,32,1536]{3,2,1,0:T(8,128)(2,1)S(1)}, bf16[1,1,32,1536]{3,2,1,0:T(8,128)(2,1)S(1)}, u32[]{:S(2)}, u32[]{:S(2)}) collective-permute-start(bf16[1,1,32,1536]{3,2,1,0:T(8,128)(2,1)S(1)} %copy-done.21), channel_id=1, source_target_pairs={{0,12},{4,16},{8,20},{12,24},{16,28},{20,0},{24,4},{28,8},{1,13},{... | collective-permute-start | bytes 294920 | tf_op jit(solution)/shard_map/ppermute | solution.py:31
  301.6 5.7 collective-permute-start.3
  301.7 7.5 %collective-permute-start.4 = (bf16[1,1,32,1536]{3,2,1,0:T(8,128)(2,1)S(1)}, bf16[1,1,32,1536]{3,2,1,0:T(8,128)(2,1)S(1)}, u32[]{:S(2)}, u32[]{:S(2)}) collective-permute-start(bf16[1,1,32,1536]{3,2,1,0:T(8,128)(2,1)S(1)} %get-tuple-element.2807), channel_id=1, source_target_pairs={{0,20},{4,24},{8,28},{12,0},{16,4},{20,8},{24,12},{28,16},{1,21},{... | collective-permute-start | bytes 294920 | tf_op jit(solution)/shard_map/ppermute | solution.py:31
  303.1 6.2 collective-permute-start.5
  304.9 4.6 collective-permute-start.6
  311.1 26.1 %all-to-all-start.2 = ((bf16[8,32,1536]{2,1,0:T(8,128)(2,1)}), bf16[8,32,1536]{2,1,0:T(8,128)(2,1)}, u32[]{:S(2)}, u32[]{:S(2)}) async-start(bf16[8,32,1536]{2,1,0:T(8,128)(2,1)} %broadcast_select_fusion.1), calls=%async_computation.2 | async-start | bytes 1572864 | tf_op jit(solution)/shard_map/all_to_all | solution.py:46
  316.5 339.3 %reduce-scatter.2.cloned.1.call-start = ((), (), s32[]{:S(2)}) async-start(), calls=%async_computation.8 | async-start | bytes 19464192 | tf_op jit(solution)/shard_map/reduce_scatter | solution.py:251
  323.3 1.5 copy-start.7
  323.3 1.5 copy-start.17
  331.2 6.0 copy-start.2
  331.2 5.1 copy-start.16
  331.2 6.1 copy-start.25
  337.2 11.0 %copy-start.18 = (bf16[1,256,1536]{2,1,0:T(8,128)(2,1)}, bf16[1,256,1536]{2,1,0:T(8,128)(2,1)S(1)}, u32[]{:S(2)}) copy-start(bf16[1,256,1536]{2,1,0:T(8,128)(2,1)S(1)} %slice.49) | copy-start | bytes 2359300
  348.3 3.9 copy-start.1
  352.2 12.7 %copy-start.3 = (f32[1024,3,128]{2,0,1:T(8,128)S(1)}, f32[1024,3,128]{2,0,1:T(8,128)}, u32[]{:S(2)}) copy-start(f32[1024,3,128]{2,0,1:T(8,128)} %copy-done.2) | copy-start | bytes 4718596
  356.4 1.4 copy-start.8
  356.4 1.4 copy-start.20
  357.8 1.4 copy-start.4
  359.9 1.1 copy-start.5
  366.6 1.9 copy-start.6
  370.1 3.4 copy-start.12
  373.5 1.4 copy-start.11
  373.6 1.8 copy-start.13
  391.3 5.2 copy-start.19
  391.3 5.2 copy-start.26
  391.3 155.0 %all-to-all-start.6 = ((bf16[2,1024,3,1,384]{4,0,3,2,1:T(2,128)(2,1)}), bf16[2,1024,3,1,384]{4,0,3,2,1:T(2,128)(2,1)}, u32[]{:S(2)}, u32[]{:S(2)}) async-start(bf16[2,1024,3,1,384]{4,0,3,2,1:T(2,128)(2,1)} %copy.284), calls=%async_computation.7 | async-start | bytes 9437184 | tf_op jit(solution)/shard_map/all_to_all | solution.py:279
Sparse Core Ops, SparseCore 0:
  348.4 307.4 reduce-scatter.1
